TPU v7x, 512 devices: a whole 4x8x8 slice. The times are simulated.
512 devices in a mesh: seq: 128 (over z, y, core), head: 4 (over x).
Axes of the slice: x: 4, y: 8, z: 8, core: 2. Of those that a mesh axis runs over, the one named last changes fastest.
Arguments:
- queries: bfloat16 [16384, 2048], P('seq', 'head'), may hold values from -1.25 to 1.25
- key_vectors: bfloat16 [16384, 2048], P('seq', 'head'), may hold values from -1.25 to 1.25
- value_vectors: bfloat16 [16384, 2048], P('seq', 'head'), may hold values from -4 to 4
- feature_proj: bfloat16 [16, 128, 256], P('head'), may hold values from -2.5 to 2.5
- out_weight: bfloat16 [2048, 2048], P('head'), may hold values from -0.1875 to 0.1875
- grad_output: bfloat16 [16384, 2048], P('seq', 'head'), may hold values from -4 to 4
Outputs:
- layer_out: bfloat16 [16384, 2048], P('seq', 'head')
- grad_queries: bfloat16 [16384, 2048], P('seq', 'head')
- grad_keys: bfloat16 [16384, 2048], P('seq', 'head')
- grad_values: bfloat16 [16384, 2048], P('seq', 'head')
All inputs are finite; a program needn't handle non-finite values.
Results may differ from a plain program's by a relative error of at most 0.025.
Values may be sent and summed in bfloat16 or wider, within the bound.
A program may use at most 128 MiB of HBM per device.

v0:
```python
import jax
import jax.numpy as jnp
from jax import lax
from jax.sharding import PartitionSpec as P

BLOCK = 128


epsilon = 1e-05


def split_up(array, dim, devices):
    shape = array.shape
    parts = array.reshape(*shape[:dim], devices, shape[dim] // devices, *shape[dim + 1 :])
    return jnp.moveaxis(parts, dim, 0)


def summed_on_arrival(array, axis, dim):
    parts = split_up(array, dim, lax.axis_size(axis))
    arrived = lax.all_to_all(parts, axis, split_axis=0, concat_axis=0, tiled=True)
    return arrived.astype(jnp.float32).sum(axis=0)


def sent_to_all(array, axis):
    copies = jnp.broadcast_to(array, (lax.axis_size(axis), *array.shape))
    return lax.all_to_all(copies, axis, split_axis=0, concat_axis=0, tiled=True)


def in_order(parts, dim):
    parts = jnp.moveaxis(parts, 0, dim)
    shape = parts.shape
    return parts.reshape(*shape[:dim], shape[dim] * shape[dim + 1], *shape[dim + 2 :])


def collect(array, axis, dim):
    parts = sent_to_all(array, axis)
    return in_order(parts, dim)


def lower_mask(width):
    row_ids = lax.broadcasted_iota(jnp.int32, (width, width), 0)
    col_ids = lax.broadcasted_iota(jnp.int32, (width, width), 1)
    return col_ids <= row_ids


def sliced_sums(total, from_end):
    flat = total.reshape(1, -1)
    spread = lax.all_to_all(flat, "seq", split_axis=1, concat_axis=0, tiled=True)
    zero_row = jnp.zeros_like(spread[:1])
    if from_end:
        summed = jnp.cumsum(spread[::-1], axis=0)[::-1]
        exclusive = jnp.concatenate([summed[1:], zero_row], axis=0)
    else:
        summed = jnp.cumsum(spread, axis=0)
        exclusive = jnp.concatenate([zero_row, summed[:-1]], axis=0)
    returned = lax.all_to_all(exclusive, "seq", split_axis=0, concat_axis=1, tiled=True)
    return returned.reshape(total.shape)


def key_states(key_feats, value_blocks):
    states = jnp.einsum(
        "hncm,hncd->hnmd", key_feats, value_blocks, preferred_element_type=jnp.float32
    )
    running = jnp.cumsum(states, axis=1)
    before_sum = jnp.concatenate([jnp.zeros_like(states), running[:, :-1]], axis=1)
    return (before_sum, running[:, -1])


def head_major(matrix, head_count, head_width):
    tok_rows = matrix.shape[0]
    return jnp.transpose(matrix.reshape(tok_rows, head_count, head_width), (1, 0, 2))


def token_major(stacked):
    head_count, tok_rows, head_width = stacked.shape
    return jnp.transpose(stacked, (1, 0, 2)).reshape(tok_rows, head_count * head_width)


def local(queries, key_vectors, value_vectors, feature_proj, out_weight, grad_output):
    head_count = feature_proj.shape[0]
    head_width = feature_proj.shape[1]
    feat_count = feature_proj.shape[2]
    tok_rows = queries.shape[0]
    n_blocks = tok_rows // BLOCK
    feat_scale = head_width ** (-0.25)
    causal = lower_mask(BLOCK)[None, None]
    q_heads = head_major(queries, head_count, head_width)
    k_heads = head_major(key_vectors, head_count, head_width)
    v_blocks = head_major(value_vectors, head_count, head_width).reshape(
        head_count, n_blocks, BLOCK, head_width
    )
    q_feat32 = jnp.exp(
        jnp.einsum("htd,hdm->htm", q_heads, feature_proj, preferred_element_type=jnp.float32)
        * feat_scale
    )
    k_wide = k_heads.astype(jnp.float32)
    half_sq = jnp.sum(k_wide * k_wide, axis=2, keepdims=True) * (feat_scale * feat_scale * 0.5)
    k_logits = jnp.einsum("htd,hdm->htm", k_heads, feature_proj, preferred_element_type=jnp.float32)
    k_feat32 = jnp.exp(k_logits * feat_scale - half_sq)
    q_feat = q_feat32.astype(jnp.bfloat16).reshape(head_count, n_blocks, BLOCK, feat_count)
    k_feat = k_feat32.astype(jnp.bfloat16).reshape(head_count, n_blocks, BLOCK, feat_count)
    before_sum, local_total = key_states(k_feat, v_blocks)
    prefix_sum = sliced_sums(local_total, False)
    carried_b = (prefix_sum[:, None] + before_sum).astype(jnp.bfloat16)
    scores = jnp.einsum("hnim,hnjm->hnij", q_feat, k_feat, preferred_element_type=jnp.float32)
    scores_b = jnp.where(causal, scores, 0.0).astype(jnp.bfloat16)
    numerator = jnp.einsum(
        "hnij,hnjd->hnid", scores_b, v_blocks, preferred_element_type=jnp.float32
    )
    numerator = numerator + jnp.einsum(
        "hnim,hnmd->hnid", q_feat, carried_b, preferred_element_type=jnp.float32
    )
    row_root = jnp.sqrt(jnp.mean(numerator * numerator, axis=3, keepdims=True) + epsilon)
    normed = numerator / row_root
    mixed = token_major(normed.astype(jnp.bfloat16).reshape(head_count, tok_rows, head_width))
    partial_out = jnp.dot(mixed, out_weight, preferred_element_type=jnp.float32)
    layer_out = summed_on_arrival(partial_out.astype(jnp.bfloat16), "head", 1).astype(jnp.bfloat16)
    grad_flat = lax.dot_general(
        collect(grad_output, "head", 1),
        out_weight,
        (((1,), (1,)), ((), ())),
        preferred_element_type=jnp.float32,
    )
    grad_mixed = head_major(grad_flat, head_count, head_width).reshape(
        head_count, n_blocks, BLOCK, head_width
    )
    grad_numer = (
        (grad_mixed - normed * jnp.mean(grad_mixed * normed, axis=3, keepdims=True)) / row_root
    ).astype(jnp.bfloat16)
    later_terms = jnp.einsum(
        "hnim,hnid->hnmd", q_feat, grad_numer, preferred_element_type=jnp.float32
    )
    backward_sum = jnp.cumsum(later_terms[:, ::-1], axis=1)[:, ::-1]
    after_local = jnp.concatenate([backward_sum[:, 1:], jnp.zeros_like(later_terms)], axis=1)
    suffix_sum = sliced_sums(backward_sum[:, 0], True)
    after_b = (suffix_sum[:, None] + after_local).astype(jnp.bfloat16)
    grad_scores = jnp.einsum(
        "hnid,hnjd->hnij", grad_numer, v_blocks, preferred_element_type=jnp.float32
    )
    grad_scores = jnp.where(causal, grad_scores, 0.0).astype(jnp.bfloat16)
    grad_v = jnp.einsum("hnij,hnid->hnjd", scores_b, grad_numer, preferred_element_type=jnp.float32)
    grad_v = grad_v + jnp.einsum(
        "hnjm,hnmd->hnjd", k_feat, after_b, preferred_element_type=jnp.float32
    )
    grad_qf = jnp.einsum("hnij,hnjm->hnim", grad_scores, k_feat, preferred_element_type=jnp.float32)
    grad_qf = grad_qf + jnp.einsum(
        "hnid,hnmd->hnim", grad_numer, carried_b, preferred_element_type=jnp.float32
    )
    grad_kf = jnp.einsum("hnij,hnim->hnjm", grad_scores, q_feat, preferred_element_type=jnp.float32)
    grad_kf = grad_kf + jnp.einsum(
        "hnjd,hnmd->hnjm", v_blocks, after_b, preferred_element_type=jnp.float32
    )
    query_terms = (grad_qf.reshape(head_count, tok_rows, feat_count) * q_feat32).astype(
        jnp.bfloat16
    )
    key_terms = (grad_kf.reshape(head_count, tok_rows, feat_count) * k_feat32).astype(jnp.bfloat16)
    grad_q = (
        jnp.einsum("htm,hdm->htd", query_terms, feature_proj, preferred_element_type=jnp.float32)
        * feat_scale
    )
    key_total = jnp.sum(key_terms.astype(jnp.float32), axis=2, keepdims=True)
    grad_k = (
        jnp.einsum("htm,hdm->htd", key_terms, feature_proj, preferred_element_type=jnp.float32)
        * feat_scale
    )
    grad_k = grad_k - key_total * k_wide * (feat_scale * feat_scale)
    return (
        layer_out,
        token_major(grad_q.astype(jnp.bfloat16)),
        token_major(grad_k.astype(jnp.bfloat16)),
        token_major(grad_v.reshape(head_count, tok_rows, head_width).astype(jnp.bfloat16)),
    )


def solution(mesh):
    placed = (
        P("seq", "head"),
        P("seq", "head"),
        P("seq", "head"),
        P("head", None, None),
        P("head", None),
        P("seq", "head"),
    )
    return jax.shard_map(
        local,
        mesh=mesh,
        in_specs=placed,
        out_specs=(P("seq", "head"), P("seq", "head"), P("seq", "head"), P("seq", "head")),
        check_vma=False,
    )
```

profile of v0, /device:TPU:1, one launch (start us, length us, event | category | flops | bytes accessed | tf_op | source)
XLA Modules:
  0.0 171.0 jit_solution(10530672047972471556)
XLA Ops:
  2.5 2.0 %fusion.27 = (bf16[4,128,256]{2,1,0:T(8,128)(2,1)S(1)}, f32[4,128,256]{2,1,0:T(8,128)}) fusion(f32[4,128]{1,0:T(4,128)S(1)} %broadcast_multiply_fusion.1, bf16[4,128,128]{1,2,0:T(8,128)(2,1)S(1)} %bitcast.141, bf16[4,128,256]{2,1,0:T(8,128)(2,1)} %param.9), kind=kOutput, calls=%fused_computation.58 | convolution fusion | flops 33947648 | bytes 1181696 | tf_op jit(solution)/shard_map/htd,hdm->htm/dot_general | solution.py:98
  5.8 38.9 %all_to_all.68 = f32[1,128,1024]{2,0,1:T(1,128)} all-to-all(f32[1,128,1024]{2,0,1:T(1,128)S(1)} %bitcast.135), channel_id=1, replica_groups=mesh['seq'=128,'head'=4] {'seq'}, dimensions={1} | all-to-all | bytes 1048576 | tf_op jit(solution)/shard_map/all_to_all | solution.py:48
  45.5 4.0 %all-to-all-start.3 = ((bf16[4,128,512]{2,1,0:T(8,128)(2,1)}), bf16[4,128,512]{2,1,0:T(8,128)(2,1)S(1)}, u32[]{:S(2)}, u32[]{:S(2)}) async-start(bf16[4,128,512]{2,1,0:T(8,128)(2,1)} %broadcast_in_dim.28), calls=%async_computation.3 | async-start | bytes 1048576 | tf_op jit(solution)/shard_map/all_to_all | solution.py:26
  50.6 2.0 %copy.134 = f32[1,128,1024]{2,1,0:T(8,128)} copy(f32[1,128,1024]{2,0,1:T(1,128)} %all_to_all.68) | data formatting | bytes 1048576
  52.6 2.2 %reduce_window_sum.24 = bf16[128,1024]{1,0:T(8,128)(2,1)} reduce-window(f32[128,1024]{1,0:T(8,128)} %bitcast.138, f32[]{:T(128)} %constant.20.clone.1), window={size=128x1 pad=127_0x0_0}, to_apply=%region_1.0 | reduce-window | flops 16646144 | bytes 786436 | tf_op jit(solution)/shard_map/jit(cumsum)/reduce_window_sum | solution.py:54
  57.0 2.4 %reduce.9 = bf16[128,1024]{1,0:T(8,128)(2,1)} reduce(bf16[128,1,1024]{2,0,1:T(8,128)(2,1)} %pad_bitcast_fusion.1, bf16[]{:T(256)} %broadcast.77), dimensions={1}, to_apply=%copy.71.reduce_sub_computation | reduce | bytes 524290 | tf_op jit(solution)/shard_map/all_to_all | solution.py:56
  59.4 1.9 %reshape.214 = bf16[128,2,512]{2,1,0:T(2,128)(2,1)} reshape(bf16[128,1024]{1,0:T(8,128)(2,1)} %reduce.9) | data formatting | bytes 524288
  61.3 6.4 %all-to-all-start.1 = ((bf16[128,2,512]{2,1,0:T(2,128)(2,1)}), bf16[128,2,512]{2,1,0:T(2,128)(2,1)}, u32[]{:S(2)}, u32[]{:S(2)}) async-start(bf16[128,2,512]{2,1,0:T(2,128)(2,1)} %reshape.214), calls=%async_computation.1 | async-start | bytes 524288 | tf_op jit(solution)/shard_map/all_to_all | solution.py:56
  70.8 2.2 %reshape.210 = bf16[128,2048,1]{1,0,2:T(8,128)(2,1)} reshape(bf16[128,4,512]{2,1,0:T(4,128)(2,1)} %copy.74) | data formatting | bytes 1048576 | tf_op jit(solution)/shard_map/reshape | solution.py:32
  73.0 9.5 %all-to-all-done.1 = bf16[128,2,512]{2,1,0:T(2,128)(2,1)} async-done(((bf16[128,2,512]{2,1,0:T(2,128)(2,1)}), bf16[128,2,512]{2,1,0:T(2,128)(2,1)}, u32[]{:S(2)}, u32[]{:S(2)}) %all-to-all-start.1) | async-done | bytes 262176 | tf_op jit(solution)/shard_map/all_to_all | solution.py:56
  82.5 2.1 %reshape.215 = bf16[128,1,1024]{2,1,0:T(2,128)(2,1)S(1)} reshape(bf16[128,2,512]{2,1,0:T(2,128)(2,1)} %all-to-all-done.1) | data formatting | bytes 524288
  84.7 2.2 %convert_reduce_fusion.2 = bf16[128,1024]{1,0:T(8,128)(2,1)} fusion(bf16[128,1,1024]{2,1,0:T(2,128)(2,1)S(1)} %reshape.215), kind=kLoop, calls=%fused_computation.34 | loop fusion | bytes 524288 | tf_op jit(solution)/shard_map/convert_element_type | solution.py:104
  92.7 6.8 %all-to-all-start.4 = ((f32[1,128,1024]{2,0,1:T(1,128)}), f32[1,128,1024]{2,0,1:T(1,128)}, u32[]{:S(2)}, u32[]{:S(2)}) async-start(f32[1,128,1024]{2,0,1:T(1,128)} %bitcast.134), calls=%async_computation.4 | async-start | bytes 1048576 | tf_op jit(solution)/shard_map/all_to_all | solution.py:48
  101.6 18.2 %all-to-all-done.4 = f32[1,128,1024]{2,0,1:T(1,128)} async-done(((f32[1,128,1024]{2,0,1:T(1,128)}), f32[1,128,1024]{2,0,1:T(1,128)}, u32[]{:S(2)}, u32[]{:S(2)}) %all-to-all-start.4) | async-done | bytes 524320 | tf_op jit(solution)/shard_map/all_to_all | solution.py:48
  119.8 4.5 %all-to-all-start.2 = ((bf16[4,128,512]{2,1,0:T(8,128)(2,1)}), bf16[4,128,512]{2,1,0:T(8,128)(2,1)}, u32[]{:S(2)}, u32[]{:S(2)}) async-start(bf16[4,128,512]{2,1,0:T(8,128)(2,1)} %bitcast.137), calls=%async_computation.2 | async-start | bytes 1048576 | tf_op jit(solution)/shard_map/all_to_all | solution.py:20
  125.2 1.9 %copy.133 = f32[1,128,1024]{2,1,0:T(8,128)} copy(f32[1,128,1024]{2,0,1:T(1,128)} %all-to-all-done.4) | data formatting | bytes 1048576
  127.2 4.7 %rev.4 = f32[128,1024]{1,0:T(8,128)} reverse(f32[128,1024]{1,0:T(8,128)} %bitcast.139), dimensions={0} | reverse | bytes 1048576 | tf_op jit(solution)/shard_map/rev | solution.py:51
  133.4 2.7 %slice.11 = bf16[127,1024]{1,0:T(8,128)(2,1)} reverse(bf16[127,1024]{1,0:T(8,128)(2,1)S(1)} %bitcast.143), dimensions={0} | reverse | bytes 520192 | tf_op jit(solution)/shard_map/slice | solution.py:52
  138.6 1.9 %reshape.216 = bf16[128,2,512]{2,1,0:T(2,128)(2,1)} reshape(bf16[128,1024]{1,0:T(8,128)(2,1)} %reduce.10) | data formatting | bytes 524288
  140.5 6.4 %all-to-all-start.5 = ((bf16[128,2,512]{2,1,0:T(2,128)(2,1)}), bf16[128,2,512]{2,1,0:T(2,128)(2,1)}, u32[]{:S(2)}, u32[]{:S(2)}) async-start(bf16[128,2,512]{2,1,0:T(2,128)(2,1)} %reshape.216), calls=%async_computation.5 | async-start | bytes 524288 | tf_op jit(solution)/shard_map/all_to_all | solution.py:56
  146.9 1.9 %fusion.28 = f32[4,128,256]{2,1,0:T(8,128)} fusion(bf16[4,128,128]{2,1,0:T(8,128)(2,1)} %fusion.13, bf16[4,128,256]{2,1,0:T(8,128)(2,1)S(1)} %get-tuple-element.24), kind=kOutput, calls=%fused_computation.59 | convolution fusion | flops 33554432 | bytes 917504 | tf_op jit(solution)/shard_map/hnij,hnjm->hnim/dot_general | solution.py:145
  154.1 7.6 %all-to-all-done.5 = bf16[128,2,512]{2,1,0:T(2,128)(2,1)} async-done(((bf16[128,2,512]{2,1,0:T(2,128)(2,1)}), bf16[128,2,512]{2,1,0:T(2,128)(2,1)}, u32[]{:S(2)}, u32[]{:S(2)}) %all-to-all-start.5) | async-done | bytes 262176 | tf_op jit(solution)/shard_map/all_to_all | solution.py:56
  161.7 2.1 %reshape.217 = bf16[128,1,1024]{2,1,0:T(2,128)(2,1)S(1)} reshape(bf16[128,2,512]{2,1,0:T(2,128)(2,1)} %all-to-all-done.5) | data formatting | bytes 524288
  163.9 2.2 %convert_reduce_fusion.1 = bf16[128,1024]{1,0:T(8,128)(2,1)} fusion(bf16[128,1,1024]{2,1,0:T(2,128)(2,1)S(1)} %reshape.217), kind=kLoop, calls=%fused_computation.32 | loop fusion | bytes 524288 | tf_op jit(solution)/shard_map/convert_element_type | solution.py:136
  (61 shorter events, 33.2 us)
Async XLA Ops:
  0.6 89.1 %copy-start = (bf16[512,2048]{1,0:T(8,128)(2,1)S(1)}, bf16[512,2048]{1,0:T(8,128)(2,1)}, u32[]{:S(2)}) copy-start(bf16[512,2048]{1,0:T(8,128)(2,1)} %param.10) | copy-start | bytes 6291460
  0.6 44.0 %copy-start.9 = (bf16[128,512]{1,0:T(8,128)(2,1)S(1)}, bf16[128,512]{1,0:T(8,128)(2,1)}, u32[]{:S(2)}) copy-start(bf16[128,512]{1,0:T(8,128)(2,1)} %param.11) | copy-start | bytes 393220
  1.9 0.7 copy-start.2
  4.5 45.0 %copy-start.1 = (bf16[4,128,256]{2,1,0:T(8,128)(2,1)S(1)}, bf16[4,128,256]{2,1,0:T(8,128)(2,1)}, u32[]{:S(2)}) copy-start(bf16[4,128,256]{2,1,0:T(8,128)(2,1)} %param.9) | copy-start | bytes 786436
  4.6 45.0 %copy-start.10 = (bf16[128,512]{1,0:T(8,128)(2,1)S(1)}, bf16[128,512]{1,0:T(8,128)(2,1)}, u32[]{:S(2)}) copy-start(bf16[128,512]{1,0:T(8,128)(2,1)} %param.6) | copy-start | bytes 393220
  45.5 15.8 %all-to-all-start.3 = ((bf16[4,128,512]{2,1,0:T(8,128)(2,1)}), bf16[4,128,512]{2,1,0:T(8,128)(2,1)S(1)}, u32[]{:S(2)}, u32[]{:S(2)}) async-start(bf16[4,128,512]{2,1,0:T(8,128)(2,1)} %broadcast_in_dim.28), calls=%async_computation.3 | async-start | bytes 1048576 | tf_op jit(solution)/shard_map/all_to_all | solution.py:26
  50.6 18.0 %copy-start.6 = (bf16[128,512]{1,0:T(8,128)(2,1)S(1)}, bf16[128,512]{1,0:T(8,128)(2,1)}, u32[]{:S(2)}) copy-start(bf16[128,512]{1,0:T(8,128)(2,1)} %param.8) | copy-start | bytes 393220
  61.3 21.2 %all-to-all-start.1 = ((bf16[128,2,512]{2,1,0:T(2,128)(2,1)}), bf16[128,2,512]{2,1,0:T(2,128)(2,1)}, u32[]{:S(2)}, u32[]{:S(2)}) async-start(bf16[128,2,512]{2,1,0:T(2,128)(2,1)} %reshape.214), calls=%async_computation.1 | async-start | bytes 524288 | tf_op jit(solution)/shard_map/all_to_all | solution.py:56
  68.0 0.6 copy-start.4
  92.7 27.1 %all-to-all-start.4 = ((f32[1,128,1024]{2,0,1:T(1,128)}), f32[1,128,1024]{2,0,1:T(1,128)}, u32[]{:S(2)}, u32[]{:S(2)}) async-start(f32[1,128,1024]{2,0,1:T(1,128)} %bitcast.134), calls=%async_computation.4 | async-start | bytes 1048576 | tf_op jit(solution)/shard_map/all_to_all | solution.py:48
  100.2 24.1 %copy-start.7 = (bf16[128,512]{1,0:T(8,128)(2,1)S(1)}, bf16[128,512]{1,0:T(8,128)(2,1)}, u32[]{:S(2)}) copy-start(bf16[128,512]{1,0:T(8,128)(2,1)} %param.8) | copy-start | bytes 393220
  119.8 20.7 %all-to-all-start.2 = ((bf16[4,128,512]{2,1,0:T(8,128)(2,1)}), bf16[4,128,512]{2,1,0:T(8,128)(2,1)}, u32[]{:S(2)}, u32[]{:S(2)}) async-start(bf16[4,128,512]{2,1,0:T(8,128)(2,1)} %bitcast.137), calls=%async_computation.2 | async-start | bytes 1048576 | tf_op jit(solution)/shard_map/all_to_all | solution.py:20
  138.6 12.7 %copy-start.8 = (bf16[4,128,128]{2,1,0:T(8,128)(2,1)S(1)}, bf16[4,128,128]{2,1,0:T(8,128)(2,1)}, u32[]{:S(2)}) copy-start(bf16[4,128,128]{2,1,0:T(8,128)(2,1)} %fusion.13) | copy-start | bytes 393220
  140.5 21.3 %all-to-all-start.5 = ((bf16[128,2,512]{2,1,0:T(2,128)(2,1)}), bf16[128,2,512]{2,1,0:T(2,128)(2,1)}, u32[]{:S(2)}, u32[]{:S(2)}) async-start(bf16[128,2,512]{2,1,0:T(2,128)(2,1)} %reshape.216), calls=%async_computation.5 | async-start | bytes 524288 | tf_op jit(solution)/shard_map/all_to_all | solution.py:56
  166.1 3.0 %copy-start.3 = (bf16[128,512]{0,1:T(8,128)(2,1)S(1)}, bf16[128,512]{0,1:T(8,128)(2,1)}, u32[]{:S(2)}) copy-start(bf16[128,512]{0,1:T(8,128)(2,1)} %copy-done.2) | copy-start | bytes 393220
  166.1 4.0 %copy-start.5 = (bf16[4,128,128]{2,1,0:T(8,128)(2,1)S(1)}, bf16[4,128,128]{2,1,0:T(8,128)(2,1)}, u32[]{:S(2)}) copy-start(bf16[4,128,128]{2,1,0:T(8,128)(2,1)} %copy-done.4) | copy-start | bytes 393220
where the time goes:
time: 173 us; the launch traced here: 171 us
  local copies, waits for them, and re-layouts  39.1 us (23%)
  blocking collectives  38.9 us (22%)
  waiting for transfers between devices  35.4 us (20%)
  starting transfers between devices  28.1 us (16%)
  matrix products  17.8 us (10%)
  other arithmetic  10.8 us (6%)
    all_to_all x1, blocking collectives, sliced_sums(): lax.all_to_all(flat, 'seq', split_axis=1, concat_axis=0, tiled=True)  38.9 us
    all_to_all x1, waiting for transfers between devices, sliced_sums(): lax.all_to_all(flat, 'seq', split_axis=1, concat_axis=0, tiled=True)  18.2 us
    all_to_all x2, waiting for transfers between devices, sliced_sums(): lax.all_to_all(exclusive, 'seq', split_axis=0, concat_axis=1, tiled=True)  17.1 us
    unnamed x32, local copies, waits for them, and re-layouts  16.8 us
    all_to_all x2, starting transfers between devices, sliced_sums(): lax.all_to_all(exclusive, 'seq', split_axis=0, concat_axis=1, tiled=True)  12.8 us
    all_to_all x1, starting transfers between devices, sliced_sums(): lax.all_to_all(flat, 'seq', split_axis=1, concat_axis=0, tiled=True)  6.76 us
    rev x1, local copies, waits for them, and re-layouts, sliced_sums(): summed = jnp.cumsum(spread[::-1], axis=0)[::-1]  4.75 us
    all_to_all x1, starting transfers between devices, summed_on_arrival(): lax.all_to_all(parts, axis, split_axis=0, concat_axis=0, tiled=True)  4.52 us
  transfers between devices with their start and end apart: 5, of which 3 were waited for; matrix products, arithmetic and copies ran while one was open for 24% of the time, Pallas kernels for 0%

commit v1 on v0

v1 whole, which is shorter than its diff:
```python
import functools
import math

import jax
import jax.numpy as jnp
from jax import lax
from jax.experimental import pallas as pl
from jax.experimental.pallas import tpu as pltpu
from jax.sharding import PartitionSpec as P

EPSILON = 1e-05
F32 = jnp.float32
BF16 = jnp.bfloat16
MESH = pl.DeviceIdType.MESH
NN = (((1,), (0,)), ((), ()))
NT = (((1,), (1,)), ((), ()))
TN = (((0,), (0,)), ((), ()))


def mm(a, b, dims):
    return lax.dot_general(a, b, dims, preferred_element_type=F32)


def far_first(n):
    return sorted(range(1, n), key=lambda d: -min(d, n - d))


def kernel(ny, nz, nx, toks, width, feats, *refs):
    (q_in, k_in, v_in, om_in, w_in, g_in,
     lo_out, gq_out, gk_out, gv_out,
     qc, kc, vc, om, w, g_all, gm,
     kf32, kf, qf32, qf, sc, gs, gn, normed, intra, kintra, vintra,
     st, p1, x2, p2, x3, total,
     mixed, mx, po, rs, lo, gq, gk, gv,
     in_sem, pair_send, pair_recv, x_send, x_recv, scan_send, scan_recv, out_sem) = refs
    me = lax.axis_index("seq")
    x = lax.axis_index("head")
    core = lax.rem(me, 2)
    y = lax.rem(lax.div(me, 2), ny)
    z = lax.div(me, 2 * ny)
    span = 2 * width
    slice_rows = feats // ny
    rows = 2 * toks
    own = pl.multiple_of(core * toks, toks)
    other = pl.multiple_of((1 - core) * toks, toks)
    own_cols = pl.multiple_of(core * span, span)
    other_cols = pl.multiple_of((1 - core) * span, span)
    scale = width ** (-0.25)

    def seq_id(zz, yy, cc):
        return {"seq": (zz * ny + yy) * 2 + cc, "head": x}

    partner = seq_id(z, y, 1 - core)
    y_peers = [lax.rem(y + d, ny) for d in far_first(ny)]
    z_peers = [lax.rem(z + d, nz) for d in far_first(nz)]
    x_peers = [lax.rem(x + d, nx) for d in far_first(nx)]

    barrier = pltpu.get_barrier_semaphore()
    peers = [partner]
    peers += [seq_id(z, yy, core) for yy in y_peers]
    peers += [seq_id(zz, y, core) for zz in z_peers]
    peers += [{"seq": me, "head": xx} for xx in x_peers]
    for peer in peers:
        pl.semaphore_signal(barrier, inc=1, device_id=peer, device_id_type=MESH)

    def fetch(src, dst, index):
        copy = pltpu.make_async_copy(src, dst, in_sem.at[index])
        copy.start()
        return copy

    own_col = pl.ds(own_cols, span)
    got_k = fetch(k_in.at[:, own_col], kc.at[pl.ds(own, toks), :], 0)
    got_om = fetch(om_in.at[pl.ds(core * 2, 2)], om, 1)
    got_q = fetch(q_in.at[:, own_col], qc.at[pl.ds(own, toks), :], 2)
    got_v = fetch(v_in.at[:, own_col], vc.at[pl.ds(own, toks), :], 3)
    got_g = fetch(g_in, g_all.at[x], 4)
    got_w = fetch(w_in, w, 5)

    def k_feats(start):
        for h in range(2):
            cols = slice(h * width, (h + 1) * width)
            kb = kc[pl.ds(start, toks), cols]
            wide = kb.astype(F32)
            half = jnp.sum(wide * wide, axis=1, keepdims=True) * (scale * scale * 0.5)
            value = jnp.exp(mm(kb, om[h], NN) * scale - half)
            kf32[h, pl.ds(start, toks), :] = value
            kf[h, pl.ds(start, toks), :] = value.astype(BF16)

    def q_feats(start):
        for h in range(2):
            cols = slice(h * width, (h + 1) * width)
            value = jnp.exp(mm(qc[pl.ds(start, toks), cols], om[h], NN) * scale)
            qf32[h, pl.ds(start, toks), :] = value
            qf[h, pl.ds(start, toks), :] = value.astype(BF16)

    got_k.wait()
    got_om.wait()
    k_feats(own)
    got_q.wait()
    q_feats(own)

    pl.semaphore_wait(barrier, len(peers))

    def to_partner(src, dst, index):
        copy = pltpu.make_async_remote_copy(
            src_ref=src, dst_ref=dst, send_sem=pair_send.at[index], recv_sem=pair_recv.at[index],
            device_id=partner, device_id_type=MESH)
        copy.start()
        return copy

    other_col = pl.ds(other_cols, span)
    own_rows = pl.ds(own, toks)
    other_rows = pl.ds(other, toks)
    sent_k = to_partner(k_in.at[:, other_col], kc.at[own_rows, :], 0)
    sent_v = to_partner(v_in.at[:, other_col], vc.at[own_rows, :], 1)
    sent_q = to_partner(q_in.at[:, other_col], qc.at[own_rows, :], 2)

    sent_g = []
    for i, xx in enumerate(x_peers):
        copy = pltpu.make_async_remote_copy(
            src_ref=g_in, dst_ref=g_all.at[x], send_sem=x_send.at[0], recv_sem=x_recv.at[0],
            device_id={"seq": me, "head": xx}, device_id_type=MESH)
        copy.start()

    got_v.wait()
    sent_k.wait_recv()
    k_feats(other)
    sent_v.wait_recv()

    def all_sent(ref, sem):
        pltpu.make_async_copy(ref, ref, sem).wait()

    class Scan:
        def __init__(self, index, backward):
            self.i, self.backward = index, backward

        def sems(self, phase, h):
            return scan_send.at[self.i, phase, h], scan_recv.at[self.i, phase, h]

        def start(self, h, state):
            i = self.i
            value = state.astype(BF16)
            for s in range(ny):
                st[i, h, s] = value[s * slice_rows:(s + 1) * slice_rows]
            ss, rr = self.sems(0, h)
            for yy in y_peers:
                pltpu.make_async_remote_copy(
                    src_ref=st.at[i, h, yy], dst_ref=p1.at[i, h, y], send_sem=ss, recv_sem=rr,
                    device_id=seq_id(z, yy, core), device_id_type=MESH).start()
            p1[i, h, y] = st[i, h, y]

        def middle(self, h):
            i = self.i
            all_sent(p1.at[i, h, pl.ds(0, ny - 1)], self.sems(0, h)[1])
            order = range(ny)[::-1] if self.backward else range(ny)
            acc = jnp.zeros((slice_rows, width), F32)
            for s in order:
                x3[i, h, s] = acc
                acc = acc + p1[i, h, s].astype(F32)
            x2[i, h] = acc.astype(BF16)
            ss, rr = self.sems(1, h)
            for zz in z_peers:
                pltpu.make_async_remote_copy(
                    src_ref=x2.at[i, h], dst_ref=p2.at[i, h, z], send_sem=ss, recv_sem=rr,
                    device_id=seq_id(zz, y, core), device_id_type=MESH).start()
            p2[i, h, z] = x2[i, h]

        def back(self, h):
            i = self.i
            all_sent(p2.at[i, h, pl.ds(0, nz - 1)], self.sems(1, h)[1])
            acc = jnp.zeros((slice_rows, width), F32)
            for s in range(nz):
                take = (s > z) if self.backward else (s < z)
                acc = acc + jnp.where(take, p2[i, h, s].astype(F32), 0.0)
            for s in range(ny):
                st[2 + i, h, s] = (x3[i, h, s] + acc).astype(BF16)
            ss, rr = self.sems(2, h)
            for yy in y_peers:
                pltpu.make_async_remote_copy(
                    src_ref=st.at[2 + i, h, yy], dst_ref=total.at[i, h, y], send_sem=ss, recv_sem=rr,
                    device_id=seq_id(z, yy, core), device_id_type=MESH).start()
            total[i, h, y] = st[2 + i, h, y]

        def result(self, h):
            i = self.i
            all_sent(total.at[i, h, pl.ds(0, ny - 1)], self.sems(2, h)[1])
            return total[i, h].reshape(feats, width)

        def finish(self):
            i = self.i
            for h in range(2):
                all_sent(p1.at[i, h, pl.ds(0, ny - 1)], self.sems(0, h)[0])
                all_sent(p2.at[i, h, pl.ds(0, nz - 1)], self.sems(1, h)[0])
                all_sent(total.at[i, h, pl.ds(0, ny - 1)], self.sems(2, h)[0])

    causal = (lax.broadcasted_iota(jnp.int32, (rows, rows), 1)
              <= lax.broadcasted_iota(jnp.int32, (rows, rows), 0))
    head_cols = [slice(h * width, (h + 1) * width) for h in range(2)]

    forward = Scan(0, False)
    for h in range(2):
        forward.start(h, mm(kf[h], vc[:, head_cols[h]], TN))

    sent_q.wait_recv()
    q_feats(other)
    for h in range(2):
        forward.middle(h)

    for h in range(2):
        scores = jnp.where(causal, mm(qf[h], kf[h], NT), 0.0).astype(BF16)
        sc[h] = scores
        intra[h] = mm(scores, vc[:, head_cols[h]], NN)
    for h in range(2):
        forward.back(h)

    got_g.wait()
    got_w.wait()
    all_sent(g_all.at[pl.ds(0, nx - 1)], x_recv.at[0])
    block = g_in.shape[1]
    grad = mm(g_all[0], w[:, 0:block], NT)
    for s in range(1, nx):
        grad = grad + mm(g_all[s], w[:, s * block:(s + 1) * block], NT)
    for c in range(2):
        gm[2 + c] = grad[:, c * span:(c + 1) * span]
    gm[core] = gm[2 + core]
    sent_gm = to_partner(gm.at[3 - core], gm.at[core], 3)
    sent_gm.wait_recv()

    backward = Scan(1, True)
    for h in range(2):
        carried = forward.result(h)
        numer = intra[h] + mm(qf[h], carried, NN)
        root = jnp.sqrt(jnp.mean(numer * numer, axis=1, keepdims=True) + EPSILON)
        unit = numer / root
        normed[h] = unit
        grad = jnp.concatenate([gm[0, :, head_cols[h]], gm[1, :, head_cols[h]]], axis=0)
        grad = (grad - unit * jnp.mean(grad * unit, axis=1, keepdims=True)) / root
        grad = grad.astype(BF16)
        gn[h] = grad
        backward.start(h, mm(qf[h], grad, TN))

    for h in range(2):
        mixed[:, head_cols[h]] = normed[h].astype(BF16)
    mx[:, own_col] = mixed[own_rows, :]
    sent_mx = to_partner(mixed.at[other_rows, :], mx.at[:, own_col], 4)

    for h in range(2):
        grad_scores = jnp.where(causal, mm(gn[h], vc[:, head_cols[h]], NT), 0.0).astype(BF16)
        gs[h] = grad_scores
    for h in range(2):
        backward.middle(h)

    sent_mx.wait_recv()
    for s in range(nx):
        po[s] = mm(mx[...], w[:, s * block:(s + 1) * block], NN).astype(BF16)
    for xx in x_peers:
        pltpu.make_async_remote_copy(
            src_ref=po.at[xx], dst_ref=rs.at[x], send_sem=x_send.at[1], recv_sem=x_recv.at[1],
            device_id={"seq": me, "head": xx}, device_id_type=MESH).start()
    rs[x] = po[x]
    for h in range(2):
        backward.back(h)

    def deliver(staged, out, index):
        keep = pltpu.make_async_copy(
            staged.at[own_rows, :], out.at[:, own_col], out_sem.at[index])
        keep.start()
        return keep, to_partner(staged.at[other_rows, :], out.at[:, own_col], 4 + index)

    for h in range(2):
        carried = total[0, h].reshape(feats, width)
        grad_qf = mm(gs[h], kf[h], NN) + mm(gn[h], carried, NT)
        terms = (grad_qf * qf32[h]).astype(BF16)
        gq[:, head_cols[h]] = (mm(terms, om[h], NT) * scale).astype(BF16)
        kintra[h] = mm(gs[h], qf[h], TN)
        vintra[h] = mm(sc[h], gn[h], TN)
    pending = [deliver(gq, gq_out, 1)]

    all_sent(rs.at[pl.ds(0, nx - 1)], x_recv.at[1])
    layer = rs[0].astype(F32)
    for s in range(1, nx):
        layer = layer + rs[s].astype(F32)
    lo[...] = layer.astype(BF16)
    lo_copy = pltpu.make_async_copy(lo, lo_out, out_sem.at[0])
    lo_copy.start()

    for h in range(2):
        after = backward.result(h)
        gv[:, head_cols[h]] = (vintra[h] + mm(kf[h], after, NN)).astype(BF16)
        grad_kf = kintra[h] + mm(vc[:, head_cols[h]], after, NT)
        terms = (grad_kf * kf32[h]).astype(BF16)
        key_total = jnp.sum(terms.astype(F32), axis=1, keepdims=True)
        grad = mm(terms, om[h], NT) * scale
        grad = grad - key_total * kc[:, head_cols[h]].astype(F32) * (scale * scale)
        gk[:, head_cols[h]] = grad.astype(BF16)
    pending.append(deliver(gv, gv_out, 2))
    pending.append(deliver(gk, gk_out, 3))

    for copy in (sent_k, sent_v, sent_q, sent_gm, sent_mx):
        copy.wait_send()
    for i in range(2):
        all_sent(rs.at[pl.ds(0, nx - 1)], x_send.at[i])
    forward.finish()
    backward.finish()
    lo_copy.wait()
    for keep, sent in pending:
        keep.wait()
        sent.wait()


def local(queries, key_vectors, value_vectors, feature_proj, out_weight, grad_output):
    toks, cols = queries.shape
    width, feats = feature_proj.shape[1:]
    nx = lax.axis_size("head")
    ny = math.isqrt(lax.axis_size("seq") // 2)
    nz = lax.axis_size("seq") // (2 * ny)
    rows, span = 2 * toks, 2 * width
    part = feats // ny
    vm = pltpu.VMEM
    scratch = [
        vm((rows, span), BF16), vm((rows, span), BF16), vm((rows, span), BF16),
        vm((2, width, feats), BF16), vm(out_weight.shape, BF16),
        vm((nx, toks, cols), BF16), vm((4, toks, span), F32),
        vm((2, rows, feats), F32), vm((2, rows, feats), BF16),
        vm((2, rows, feats), F32), vm((2, rows, feats), BF16),
        vm((2, rows, rows), BF16), vm((2, rows, rows), BF16),
        vm((2, rows, width), BF16), vm((2, rows, width), F32),
        vm((2, rows, width), F32), vm((2, rows, feats), F32),
        vm((2, rows, width), F32),
        vm((4, 2, ny, part, width), BF16), vm((2, 2, ny, part, width), BF16),
        vm((2, 2, part, width), BF16), vm((2, 2, nz, part, width), BF16),
        vm((2, 2, ny, part, width), F32), vm((2, 2, ny, part, width), BF16),
        vm((rows, span), BF16), vm((toks, cols), BF16),
        vm((nx, toks, cols), BF16), vm((nx, toks, cols), BF16),
        vm((toks, cols), BF16), vm((rows, span), BF16),
        vm((rows, span), BF16), vm((rows, span), BF16),
        pltpu.SemaphoreType.DMA((6,)), pltpu.SemaphoreType.DMA((8,)),
        pltpu.SemaphoreType.DMA((8,)), pltpu.SemaphoreType.DMA((2,)),
        pltpu.SemaphoreType.DMA((2,)), pltpu.SemaphoreType.DMA((2, 3, 2)),
        pltpu.SemaphoreType.DMA((2, 3, 2)), pltpu.SemaphoreType.DMA((4,)),
    ]
    out = jax.ShapeDtypeStruct((toks, cols), BF16)
    return pl.pallas_call(
        functools.partial(kernel, ny, nz, nx, toks, width, feats),
        out_shape=(out,) * 4,
        in_specs=[pl.BlockSpec(memory_space=pl.ANY)] * 6,
        out_specs=(pl.BlockSpec(memory_space=pl.ANY),) * 4,
        scratch_shapes=scratch,
        compiler_params=pltpu.CompilerParams(collective_id=0, has_side_effects=True),
    )(queries, key_vectors, value_vectors, feature_proj, out_weight, grad_output)


def solution(mesh):
    rows = P("seq", "head")
    return jax.shard_map(
        local,
        mesh=mesh,
        in_specs=(rows, rows, rows, P("head", None, None), P("head", None), rows),
        out_specs=(rows,) * 4,
        check_vma=False,
    )
```

time: 173 us -> 54.8 us (0.32); the launches traced: 171 us -> 54.6 us
  Pallas kernels: 0 us -> 47.7 us
  blocking collectives: 38.9 us -> 0 us
  waiting for transfers between devices: 35.4 us -> 0 us
  local copies, waits for them, and re-layouts: 39.1 us -> 6.27 us
  starting transfers between devices: 28.1 us -> 0 us
  matrix products: 17.8 us -> 0 us
  other arithmetic: 10.8 us -> 0 us
    pallas_call x0 -> x1, Pallas kernels: none -> 47.7 us  [local(): pl.pallas_call(functools.partial(kernel, ny, nz, nx, toks, width, feats),...]
    all_to_all x1 -> x0, blocking collectives: 38.9 us -> none  [sliced_sums(): lax.all_to_all(flat, 'seq', split_axis=1, concat_axis=0, tiled=True)]
    all_to_all x5 -> x0, waiting for transfers between devices: 35.4 us -> none  [the longest x1 18.2 us: sliced_sums(): lax.all_to_all(flat, 'seq', split_axis=1, concat_axis=0, tiled=True)]
    all_to_all x5 -> x0, starting transfers between devices: 28.1 us -> none  [the longest x2 12.8 us: sliced_sums(): lax.all_to_all(exclusive, 'seq', split_axis=0, concat_axis=1, tiled=True)]
    dot_general x17 -> x0, matrix products: 17.8 us -> none  [the longest x1 2.04 us: local(): jnp.einsum('htd,hdm->htm', k_heads, feature_proj, preferred_element_type=...]
    unnamed x32 -> x4, local copies, waits for them, and re-layouts: 16.8 us -> 6.27 us
    convert_element_type x4 -> x0, local copies, waits for them, and re-layouts: 6.54 us -> none  [the longest x2 3.3 us: local(): after_b = (suffix_sum[:, None] + after_local).astype(jnp.bfloat16)]
    rev x1 -> x0, local copies, waits for them, and re-layouts: 4.75 us -> none  [sliced_sums(): summed = jnp.cumsum(spread[::-1], axis=0)[::-1]]
  transfers between devices with their start and end apart: 5 -> 0, of which waited for: 3 -> 0; matrix products, arithmetic and copies ran while one was open for 24% -> 0% of each run, Pallas kernels for 0% -> 0%
where the time goes in v1:
time: 54.8 us; the launch traced here: 54.6 us
  Pallas kernels  47.7 us (87%)
  local copies, waits for them, and re-layouts  6.27 us (11%)
  between operations  0.64 us (1%)
    pallas_call x1, Pallas kernels, local(): pl.pallas_call(functools.partial(kernel, ny, nz, nx, toks, width, feats),...  47.7 us
    unnamed x4, local copies, waits for them, and re-layouts  6.27 us

profile of v1, /device:TPU:1, one launch (start us, length us, event | category | flops | bytes accessed | tf_op | source)
XLA Modules:
  0.0 54.6 jit_solution(2781643208034050272)
XLA Ops:
  0.6 47.7 %shard_map.93 = (bf16[128,512]{1,0:T(8,128)(2,1)}, bf16[128,512]{1,0:T(8,128)(2,1)}, bf16[128,512]{1,0:T(8,128)(2,1)}, bf16[128,512]{1,0:T(8,128)(2,1)}) custom-call(bf16[128,512]{1,0:T(8,128)(2,1)} %refs_0_.1, bf16[128,512]{1,0:T(8,128)(2,1)} %refs_1_.1, bf16[128,512]{1,0:T(8,128)(2,1)} %refs_2_.1, bf16[4,128,256]{2,1,0:T(8,128)(2,1)} %refs_3_.1, ...), custom_call_target="tpu_custom_call" | custom-call | tf_op jit(solution)/shard_map/pallas_call | solution.py:343
  48.4 1.6 %copy.14 = bf16[128,512]{1,0:T(8,128)(2,1)} copy(bf16[128,512]{1,0:T(8,128)(2,1)} %get-tuple-element.8) | data formatting | bytes 262144
  49.9 1.6 %copy.15 = bf16[128,512]{1,0:T(8,128)(2,1)} copy(bf16[128,512]{1,0:T(8,128)(2,1)} %get-tuple-element.9) | data formatting | bytes 262144
  51.5 1.6 %copy.16 = bf16[128,512]{1,0:T(8,128)(2,1)} copy(bf16[128,512]{1,0:T(8,128)(2,1)} %get-tuple-element.10) | data formatting | bytes 262144
  53.1 1.6 %copy.17 = bf16[128,512]{1,0:T(8,128)(2,1)} copy(bf16[128,512]{1,0:T(8,128)(2,1)} %get-tuple-element.11) | data formatting | bytes 262144

commit v2 on v1

--- a/solution.py
+++ b/solution.py
@@ -31,7 +31,7 @@
      qc, kc, vc, om, w, g_all, gm,
      kf32, kf, qf32, qf, sc, gs, gn, normed, intra, kintra, vintra,
      st, p1, x2, p2, x3, total,
-     mixed, mx, po, rs, lo, gq, gk, gv,
+     mixed, mx, po, rs, gq, gk, gv,
      in_sem, pair_send, pair_recv, x_send, x_recv, scan_send, scan_recv, out_sem) = refs
     me = lax.axis_index("seq")
     x = lax.axis_index("head")
@@ -280,9 +280,7 @@
     layer = rs[0].astype(F32)
     for s in range(1, nx):
         layer = layer + rs[s].astype(F32)
-    lo[...] = layer.astype(BF16)
-    lo_copy = pltpu.make_async_copy(lo, lo_out, out_sem.at[0])
-    lo_copy.start()
+    lo_out[...] = layer.astype(BF16)
 
     for h in range(2):
         after = backward.result(h)
@@ -302,10 +300,17 @@
         all_sent(rs.at[pl.ds(0, nx - 1)], x_send.at[i])
     forward.finish()
     backward.finish()
-    lo_copy.wait()
     for keep, sent in pending:
         keep.wait()
         sent.wait()
+
+
+def write_out(*refs):
+    copies = [pltpu.make_async_copy(refs[i], refs[4 + i], refs[8].at[i]) for i in range(4)]
+    for copy in copies:
+        copy.start()
+    for copy in copies:
+        copy.wait()
 
 
 def local(queries, key_vectors, value_vectors, feature_proj, out_weight, grad_output):
@@ -332,22 +337,30 @@
         vm((2, 2, ny, part, width), F32), vm((2, 2, ny, part, width), BF16),
         vm((rows, span), BF16), vm((toks, cols), BF16),
         vm((nx, toks, cols), BF16), vm((nx, toks, cols), BF16),
-        vm((toks, cols), BF16), vm((rows, span), BF16),
-        vm((rows, span), BF16), vm((rows, span), BF16),
+        vm((rows, span), BF16), vm((rows, span), BF16), vm((rows, span), BF16),
         pltpu.SemaphoreType.DMA((6,)), pltpu.SemaphoreType.DMA((8,)),
         pltpu.SemaphoreType.DMA((8,)), pltpu.SemaphoreType.DMA((2,)),
         pltpu.SemaphoreType.DMA((2,)), pltpu.SemaphoreType.DMA((2, 3, 2)),
         pltpu.SemaphoreType.DMA((2, 3, 2)), pltpu.SemaphoreType.DMA((4,)),
     ]
     out = jax.ShapeDtypeStruct((toks, cols), BF16)
-    return pl.pallas_call(
+    held = pltpu.VMEM((toks, cols), BF16)
+    staged = pl.pallas_call(
         functools.partial(kernel, ny, nz, nx, toks, width, feats),
-        out_shape=(out,) * 4,
+        out_shape=(held,) * 4,
         in_specs=[pl.BlockSpec(memory_space=pl.ANY)] * 6,
-        out_specs=(pl.BlockSpec(memory_space=pl.ANY),) * 4,
+        out_specs=(pl.BlockSpec(memory_space=pltpu.VMEM),) * 4,
         scratch_shapes=scratch,
         compiler_params=pltpu.CompilerParams(collective_id=0, has_side_effects=True),
     )(queries, key_vectors, value_vectors, feature_proj, out_weight, grad_output)
+    return pl.pallas_call(
+        write_out,
+        out_shape=(out,) * 4,
+        in_specs=[pl.BlockSpec(memory_space=pl.ANY)] * 4,
+        compiler_params=pltpu.CompilerParams(vmem_limit_bytes=1 << 20),
+        out_specs=(pl.BlockSpec(memory_space=pl.ANY),) * 4,
+        scratch_shapes=[pltpu.SemaphoreType.DMA((4,))],
+    )(*staged)
 
 
 def solution(mesh):

time: 54.8 us -> 49.2 us (0.90)
  local copies, waits for them, and re-layouts: 6.27 us -> 0 us
  Pallas kernels: 47.7 us -> 48.4 us
    unnamed x4 -> x0, local copies, waits for them, and re-layouts: 6.27 us -> none
    pallas_call x0 -> x1, Pallas kernels: none -> 0.82 us  [local(): pl.pallas_call(write_out, out_shape=(out,) * 4, in_specs=[pl.BlockSpec(me...]
where the time goes in v2:
time: 49.2 us; the launch traced here: 49.1 us
  Pallas kernels  48.4 us (98%)
  between operations  0.64 us (1%)
    pallas_call x1, Pallas kernels, local(): pl.pallas_call(functools.partial(kernel, ny, nz, nx, toks, width, feats),...  47.6 us

profile of v2, /device:TPU:1, one launch (start us, length us, event | category | flops | bytes accessed | tf_op | source)
XLA Modules:
  0.0 49.1 jit_solution(9024099276674036175)
XLA Ops:
  0.6 47.6 %shard_map.93 = (bf16[128,512]{1,0:T(8,128)(2,1)S(1)}, bf16[128,512]{1,0:T(8,128)(2,1)S(1)}, bf16[128,512]{1,0:T(8,128)(2,1)S(1)}, bf16[128,512]{1,0:T(8,128)(2,1)S(1)}) custom-call(bf16[128,512]{1,0:T(8,128)(2,1)} %refs_0_.1, bf16[128,512]{1,0:T(8,128)(2,1)} %refs_1_.1, bf16[128,512]{1,0:T(8,128)(2,1)} %refs_2_.1, bf16[4,128,256]{2,1,0:T(8,128)(2,1)} %refs_3_.1, ...), custom_call_target="tpu_custom_call" | custom-call | tf_op jit(solution)/shard_map/pallas_call | solution.py:348
  48.2 0.8 %shard_map.94 = (bf16[128,512]{1,0:T(8,128)(2,1)}, bf16[128,512]{1,0:T(8,128)(2,1)}, bf16[128,512]{1,0:T(8,128)(2,1)}, bf16[128,512]{1,0:T(8,128)(2,1)}) custom-call(bf16[128,512]{1,0:T(8,128)(2,1)S(1)} %get-tuple-element.8.refs_0_, bf16[128,512]{1,0:T(8,128)(2,1)S(1)} %get-tuple-element.9.refs_1_, bf16[128,512]{1,0:T(8,128)(2,1)S(1)} %get-tuple-element.10.refs_2_, ...), custom_call_target="tpu_custom_call" | custom-call | tf_op jit(solution)/shard_map/pallas_call | solution.py:356

commit v3 on v2

v3 whole, which is shorter than its diff:
```python
import functools
import itertools
import math

import jax
import jax.numpy as jnp
from jax import lax
from jax.experimental import pallas as pl
from jax.experimental.pallas import tpu as pltpu
from jax.sharding import PartitionSpec as P

EPSILON = 1e-05
F32 = jnp.float32
BF16 = jnp.bfloat16
MESH = pl.DeviceIdType.MESH
NN = (((1,), (0,)), ((), ()))
NT = (((1,), (1,)), ((), ()))
TN = (((0,), (0,)), ((), ()))


def mm(a, b, dims):
    return lax.dot_general(a, b, dims, preferred_element_type=F32)


def far_first(n):
    return sorted(range(1, n), key=lambda d: -min(d, n - d))


def kernel(ny, nz, nx, toks, width, feats, *refs):
    (q_in, k_in, v_in, om_in, w_in, g_in,
     lo_out, gq_out, gk_out, gv_out,
     qc, kc, vc, ko, vo, om, omo, w, g_all, gm,
     kf32, kf, qf32, qf, sc, gs, gn, normed, intra, kintra, vintra,
     st, p1, x2, p2, x3, total,
     mixed, mx, po, rs, gq, gk, gv, mine, away, got, qft, omt,
     direct, pd, pf, tother, kfo, kfo32, kio, vio, omto,
     in_sem, pair_send, pair_recv, x_send, x_recv, scan_send, scan_recv, both_sem) = refs
    me = lax.axis_index("seq")
    x = lax.axis_index("head")
    core = lax.rem(me, 2)
    y = lax.rem(lax.div(me, 2), ny)
    z = lax.div(me, 2 * ny)
    span = 2 * width
    slice_rows = feats // ny
    rows = 2 * toks
    own = pl.multiple_of(core * toks, toks)
    other = pl.multiple_of((1 - core) * toks, toks)
    own_cols = pl.multiple_of(core * span, span)
    other_cols = pl.multiple_of((1 - core) * span, span)
    scale = width ** (-0.25)

    def seq_id(zz, yy, cc):
        return {"seq": (zz * ny + yy) * 2 + cc, "head": x}

    partner = seq_id(z, y, 1 - core)
    y_peers = [lax.rem(y + d, ny) for d in far_first(ny)]
    z_peers = [lax.rem(z + d, nz) for d in far_first(nz)]
    x_peers = [lax.rem(x + d, nx) for d in far_first(nx)]

    barrier = pltpu.get_barrier_semaphore()
    peers = []
    for yy, zz in itertools.zip_longest(y_peers, z_peers):
        if yy is not None:
            peers.append(seq_id(z, yy, core))
            peers.append(seq_id(z, yy, 1 - core))
        if zz is not None:
            peers.append(seq_id(zz, y, core))
    peers += [{"seq": me, "head": xx} for xx in x_peers] + [partner]
    for peer in peers:
        pl.semaphore_signal(barrier, inc=1, device_id=peer, device_id_type=MESH)

    def fetch(src, dst, index):
        copy = pltpu.make_async_copy(src, dst, in_sem.at[index])
        copy.start()
        return copy

    own_col = pl.ds(own_cols, span)
    got_k = fetch(k_in.at[:, own_col], kc.at[pl.ds(own, toks), :], 0)
    got_om = fetch(om_in.at[pl.ds(core * 2, 2)], om, 1)
    got_q = fetch(q_in.at[:, own_col], qc.at[pl.ds(own, toks), :], 2)
    got_v = fetch(v_in.at[:, own_col], vc.at[pl.ds(own, toks), :], 3)
    other_col = pl.ds(other_cols, span)
    got_ko = fetch(k_in.at[:, other_col], ko, 6)
    got_omo = fetch(om_in.at[pl.ds((1 - core) * 2, 2)], omo, 7)
    got_vo = fetch(v_in.at[:, other_col], vo, 8)
    got_g = fetch(g_in, g_all.at[x], 4)
    got_w = fetch(w_in, w, 5)

    def key_feature(kb, omega):
        wide = kb.astype(F32)
        half = jnp.sum(wide * wide, axis=1, keepdims=True) * (scale * scale * 0.5)
        return jnp.exp(mm(kb, omega, NN) * scale - half)

    def k_feats(start):
        for h in range(2):
            value = key_feature(kc[pl.ds(start, toks), h * width:(h + 1) * width], om[h])
            kf32[h, pl.ds(start, toks), :] = value
            kf[h, pl.ds(start, toks), :] = value.astype(BF16)

    def q_feats(start):
        for h in range(2):
            cols = slice(h * width, (h + 1) * width)
            value = jnp.exp(mm(qc[pl.ds(start, toks), cols], om[h], NN) * scale)
            qf32[h, pl.ds(start, toks), :] = value
            qf[h, pl.ds(start, toks), :] = value.astype(BF16)

    def put_slices(ref, index, state):
        value = state.astype(BF16)
        for s in range(ny):
            ref[index, s] = value[s * slice_rows:(s + 1) * slice_rows]

    got_k.wait()
    got_om.wait()
    k_feats(own)
    got_v.wait()
    own_rows = pl.ds(own, toks)
    other_rows = pl.ds(other, toks)
    head_cols = [slice(h * width, (h + 1) * width) for h in range(2)]
    got_ko.wait()
    got_omo.wait()
    got_vo.wait()
    for h in range(2):
        feature = key_feature(ko[:, head_cols[h]], omo[h])
        if h == 1:
            kfo32[...] = feature
        feature = feature.astype(BF16)
        if h == 0:
            put_slices(direct, 1 - core, mm(feature, vo[:, head_cols[h]], TN))
        else:
            kfo[...] = feature
            away[...] = mm(feature, vo[:, head_cols[h]], TN).astype(BF16)
    put_slices(direct, core, mm(kf[0, own_rows, :], vc[own_rows, head_cols[0]], TN))
    mine[...] = mm(kf[1, own_rows, :], vc[own_rows, head_cols[1]], TN)
    pl.semaphore_wait(barrier, len(peers))

    def to_partner(src, dst, index):
        copy = pltpu.make_async_remote_copy(
            src_ref=src, dst_ref=dst, send_sem=pair_send.at[index], recv_sem=pair_recv.at[index],
            device_id=partner, device_id_type=MESH)
        copy.start()
        return copy

    sent_away = to_partner(away, got, 0)
    def all_sent(ref, sem):
        pltpu.make_async_copy(ref, ref, sem).wait()

    class Scan:
        def __init__(self, index, backward):
            self.i, self.backward = index, backward

        def sems(self, phase, h):
            return scan_send.at[self.i, phase, h], scan_recv.at[self.i, phase, h]

        def start(self, h, state):
            i = self.i
            put_slices(st.at[i], h, state)
            ss, rr = self.sems(0, h)
            for yy in y_peers:
                pltpu.make_async_remote_copy(
                    src_ref=st.at[i, h, yy], dst_ref=p1.at[i, h, y], send_sem=ss, recv_sem=rr,
                    device_id=seq_id(z, yy, core), device_id_type=MESH).start()
            p1[i, h, y] = st[i, h, y]

        def start_direct(self):
            ss, rr = self.sems(0, 0)
            for yy in y_peers:
                for cc in (core, 1 - core):
                    pltpu.make_async_remote_copy(
                        src_ref=direct.at[cc, yy], dst_ref=pd.at[core * ny + y], send_sem=ss, recv_sem=rr,
                        device_id=seq_id(z, yy, cc), device_id_type=MESH).start()
            pltpu.make_async_remote_copy(
                src_ref=direct.at[1 - core, y], dst_ref=pd.at[core * ny + y], send_sem=ss, recv_sem=rr,
                device_id=partner, device_id_type=MESH).start()
            pd[core * ny + y] = direct[core, y]

        def merge(self):
            ss, rr = self.sems(0, 0)
            all_sent(pd.at[pl.ds(0, 2 * ny - 1)], rr)
            for s in range(ny):
                pf[s] = pd[s].astype(F32) + pd[ny + s].astype(F32)

        def middle(self, h):
            i = self.i
            swapped = (i, h) == (0, 0)
            if swapped:
                self.merge()
            else:
                all_sent(p1.at[i, h, pl.ds(0, ny - 1)], self.sems(0, h)[1])

            def term(s):
                return pf[s] if swapped else p1[i, h, s].astype(F32)

            acc = term(0)
            for s in range(1, ny):
                acc = acc + term(s)
            x2[i, h] = acc.astype(BF16)
            ss, rr = self.sems(1, h)
            for zz in z_peers:
                pltpu.make_async_remote_copy(
                    src_ref=x2.at[i, h], dst_ref=p2.at[i, h, z], send_sem=ss, recv_sem=rr,
                    device_id=seq_id(zz, y, core), device_id_type=MESH).start()
            p2[i, h, z] = x2[i, h]
            order = range(ny)[::-1] if self.backward else range(ny)
            acc = jnp.zeros((slice_rows, width), F32)
            for s in order:
                x3[i, h, s] = acc
                acc = acc + term(s)

        def back(self, h):
            i = self.i
            all_sent(p2.at[i, h, pl.ds(0, nz - 1)], self.sems(1, h)[1])
            acc = jnp.zeros((slice_rows, width), F32)
            for s in range(nz):
                take = (s > z) if self.backward else (s < z)
                acc = acc + jnp.where(take, p2[i, h, s].astype(F32), 0.0)
            ss, rr = self.sems(2, h)
            for yy in y_peers:
                st[2 + i, h, yy] = (x3[i, h, yy] + acc).astype(BF16)
                pltpu.make_async_remote_copy(
                    src_ref=st.at[2 + i, h, yy], dst_ref=total.at[i, h, y], send_sem=ss, recv_sem=rr,
                    device_id=seq_id(z, yy, core), device_id_type=MESH).start()
                if (i, h) == (1, 1):
                    self.both(seq_id(z, yy, 1 - core), yy)
            st[2 + i, h, y] = (x3[i, h, y] + acc).astype(BF16)
            total[i, h, y] = st[2 + i, h, y]
            if (i, h) == (1, 1):
                self.both(partner, y)

        def both(self, device, yy):
            pltpu.make_async_remote_copy(
                src_ref=st.at[3, 1, yy], dst_ref=tother.at[y], send_sem=both_sem.at[0],
                recv_sem=both_sem.at[1], device_id=device, device_id_type=MESH).start()

        def result(self, h):
            i = self.i
            all_sent(total.at[i, h, pl.ds(0, ny - 1)], self.sems(2, h)[1])
            return total[i, h].reshape(feats, width)

        def finish(self):
            i = self.i
            for h in range(2):
                if (i, h) == (0, 0):
                    all_sent(pd.at[pl.ds(0, 2 * ny - 1)], self.sems(0, h)[0])
                else:
                    all_sent(p1.at[i, h, pl.ds(0, ny - 1)], self.sems(0, h)[0])
                all_sent(p2.at[i, h, pl.ds(0, nz - 1)], self.sems(1, h)[0])
                all_sent(total.at[i, h, pl.ds(0, ny - 1)], self.sems(2, h)[0])

    causal = (lax.broadcasted_iota(jnp.int32, (rows, rows), 1)
              <= lax.broadcasted_iota(jnp.int32, (rows, rows), 0))
    forward = Scan(0, False)
    forward.start_direct()
    sent_away.wait_recv()
    forward.start(1, mine[...] + got[...].astype(F32))

    sent_k = to_partner(k_in.at[:, other_col], kc.at[own_rows, :], 2)
    sent_v = to_partner(v_in.at[:, other_col], vc.at[own_rows, :], 3)
    sent_q = to_partner(q_in.at[:, other_col], qc.at[own_rows, :], 4)

    for i, xx in enumerate(x_peers):
        copy = pltpu.make_async_remote_copy(
            src_ref=g_in, dst_ref=g_all.at[x], send_sem=x_send.at[0], recv_sem=x_recv.at[0],
            device_id={"seq": me, "head": xx}, device_id_type=MESH)
        copy.start()

    got_q.wait()
    q_feats(own)
    sent_k.wait_recv()
    k_feats(other)
    sent_q.wait_recv()
    q_feats(other)
    sent_v.wait_recv()
    for h in range(2):
        forward.middle(h)
    for h in range(2):
        qft[h] = qf[h].T
        omt[h] = om[h].T
    omto[...] = omo[1].T

    for h in range(2):
        scores = jnp.where(causal, mm(qf[h], kf[h], NT), 0.0).astype(BF16)
        sc[h] = scores
        intra[h] = mm(scores, vc[:, head_cols[h]], NN)
    for h in range(2):
        forward.back(h)

    got_g.wait()
    got_w.wait()
    all_sent(g_all.at[pl.ds(0, nx - 1)], x_recv.at[0])
    block = g_in.shape[1]
    grad = mm(g_all[0], w[:, 0:block], NT)
    for s in range(1, nx):
        grad = grad + mm(g_all[s], w[:, s * block:(s + 1) * block], NT)
    for c in range(2):
        gm[2 + c] = grad[:, c * span:(c + 1) * span]
    gm[core] = gm[2 + core]
    sent_gm = to_partner(gm.at[3 - core], gm.at[core], 5)
    sent_gm.wait_recv()

    backward = Scan(1, True)
    for h in range(2):
        carried = forward.result(h)
        numer = intra[h] + mm(qf[h], carried, NN)
        root = jnp.sqrt(jnp.mean(numer * numer, axis=1, keepdims=True) + EPSILON)
        unit = numer / root
        normed[h] = unit
        grad = jnp.concatenate([gm[0, :, head_cols[h]], gm[1, :, head_cols[h]]], axis=0)
        grad = (grad - unit * jnp.mean(grad * unit, axis=1, keepdims=True)) / root
        grad = grad.astype(BF16)
        gn[h] = grad
        backward.start(h, mm(qft[h], grad, NN))

    for h in range(2):
        mixed[:, head_cols[h]] = normed[h].astype(BF16)
    mx[:, own_col] = mixed[own_rows, :]
    sent_mx = to_partner(mixed.at[other_rows, :], mx.at[:, own_col], 6)

    for h in range(2):
        grad_scores = jnp.where(causal, mm(gn[h], vc[:, head_cols[h]], NT), 0.0).astype(BF16)
        gs[h] = grad_scores
    for h in range(2):
        backward.middle(h)

    sent_mx.wait_recv()
    for s in range(nx):
        po[s] = mm(mx[...], w[:, s * block:(s + 1) * block], NN).astype(BF16)
    for xx in x_peers:
        pltpu.make_async_remote_copy(
            src_ref=po.at[xx], dst_ref=rs.at[x], send_sem=x_send.at[1], recv_sem=x_recv.at[1],
            device_id={"seq": me, "head": xx}, device_id_type=MESH).start()
    rs[x] = po[x]
    for h in range(2):
        backward.back(h)

    pending = []

    def deliver(staged, out, h, index):
        pending.append(to_partner(staged.at[h, other_rows, :], out.at[core * 2 + h], 7 + 2 * index + h))

    for h in range(2):
        carried = total[0, h].reshape(feats, width)
        grad_qf = mm(gs[h], kf[h], NN) + mm(gn[h], carried, NT)
        terms = (grad_qf * qf32[h]).astype(BF16)
        gq[h] = (mm(terms, om[h], NT) * scale).astype(BF16)
        deliver(gq, gq_out, h, 0)
        gq_out[core * 2 + h] = gq[h, own_rows, :]
        kintra[h] = mm(gs[h], qf[h], TN)
        vintra[h] = mm(sc[h], gn[h], TN)
    sent_intra = [
        to_partner(kintra.at[1, other_rows, :], kio, 10),
        to_partner(vintra.at[1, other_rows, :], vio, 1),
    ]

    all_sent(rs.at[pl.ds(0, nx - 1)], x_recv.at[1])
    layer = rs[0].astype(F32)
    for s in range(1, nx):
        layer = layer + rs[s].astype(F32)
    lo_out[...] = layer.astype(BF16)

    def key_side(value_part, key_part, feature32, feature, values, keys, omega_t, after):
        grad_v = (value_part + mm(feature, after, NN)).astype(BF16)
        grad_kf = key_part + mm(values, after, NT)
        terms = (grad_kf * feature32).astype(BF16)
        key_total = jnp.sum(terms.astype(F32), axis=1, keepdims=True)
        grad = mm(terms, omega_t, NN) * scale
        grad = grad - key_total * keys.astype(F32) * (scale * scale)
        return grad_v, grad.astype(BF16)

    def own_head(h, after, rows):
        return key_side(
            vintra[h, rows, :], kintra[h, rows, :], kf32[h, rows, :], kf[h, rows, :],
            vc[rows, head_cols[h]], kc[rows, head_cols[h]], omt[h], after)

    after = backward.result(0)
    gv[0, other_rows, :], gk[0, other_rows, :] = own_head(0, after, other_rows)
    deliver(gv, gv_out, 0, 1)
    deliver(gk, gk_out, 0, 2)
    gv_out[core * 2], gk_out[core * 2] = own_head(0, after, own_rows)
    after = backward.result(1)
    gv_out[core * 2 + 1], gk_out[core * 2 + 1] = own_head(1, after, own_rows)
    for copy in sent_intra:
        copy.wait_recv()
    all_sent(tother, both_sem.at[1])
    away_head = (1 - core) * 2 + 1
    gv_out[away_head], gk_out[away_head] = key_side(
        vio[...], kio[...], kfo32[...], kfo[...], vo[:, head_cols[1]], ko[:, head_cols[1]],
        omto[...], tother[...].reshape(feats, width))
    all_sent(tother, both_sem.at[0])
    for copy in sent_intra:
        copy.wait_send()

    for copy in (sent_away, sent_k, sent_v, sent_q, sent_gm, sent_mx):
        copy.wait_send()
    for i in range(2):
        all_sent(rs.at[pl.ds(0, nx - 1)], x_send.at[i])
    forward.finish()
    backward.finish()
    for copy in pending:
        copy.wait()


def write_out(heads, width, lo, gq, gk, gv, lo_out, gq_out, gk_out, gv_out, sem):
    copies = [pltpu.make_async_copy(lo, lo_out, sem.at[0])]
    for i, (held, out) in enumerate(((gq, gq_out), (gk, gk_out), (gv, gv_out))):
        for h in range(heads):
            copies.append(pltpu.make_async_copy(
                held.at[h], out.at[:, pl.ds(h * width, width)], sem.at[1 + heads * i + h]))
    for copy in copies:
        copy.start()
    for copy in copies:
        copy.wait()


def local(queries, key_vectors, value_vectors, feature_proj, out_weight, grad_output):
    toks, cols = queries.shape
    width, feats = feature_proj.shape[1:]
    nx = lax.axis_size("head")
    ny = math.isqrt(lax.axis_size("seq") // 2)
    nz = lax.axis_size("seq") // (2 * ny)
    rows, span = 2 * toks, 2 * width
    part = feats // ny
    vm = pltpu.VMEM
    scratch = [
        vm((rows, span), BF16), vm((rows, span), BF16), vm((rows, span), BF16),
        vm((toks, span), BF16), vm((toks, span), BF16),
        vm((2, width, feats), BF16), vm((2, width, feats), BF16),
        vm(out_weight.shape, BF16),
        vm((nx, toks, cols), BF16), vm((4, toks, span), F32),
        vm((2, rows, feats), F32), vm((2, rows, feats), BF16),
        vm((2, rows, feats), F32), vm((2, rows, feats), BF16),
        vm((2, rows, rows), BF16), vm((2, rows, rows), BF16),
        vm((2, rows, width), BF16), vm((2, rows, width), F32),
        vm((2, rows, width), F32), vm((2, rows, feats), F32),
        vm((2, rows, width), F32),
        vm((4, 2, ny, part, width), BF16), vm((2, 2, ny, part, width), BF16),
        vm((2, 2, part, width), BF16), vm((2, 2, nz, part, width), BF16),
        vm((2, 2, ny, part, width), F32), vm((2, 2, ny, part, width), BF16),
        vm((rows, span), BF16), vm((toks, cols), BF16),
        vm((nx, toks, cols), BF16), vm((nx, toks, cols), BF16),
        vm((2, rows, width), BF16), vm((2, rows, width), BF16),
        vm((2, rows, width), BF16), vm((feats, width), F32),
        vm((feats, width), BF16), vm((feats, width), BF16),
        vm((2, feats, rows), BF16), vm((2, feats, width), BF16),
        vm((2, ny, part, width), BF16), vm((2 * ny, part, width), BF16),
        vm((ny, part, width), F32), vm((ny, part, width), BF16),
        vm((toks, feats), BF16), vm((toks, feats), F32),
        vm((toks, feats), F32), vm((toks, width), F32),
        vm((feats, width), BF16),
        pltpu.SemaphoreType.DMA((9,)), pltpu.SemaphoreType.DMA((13,)),
        pltpu.SemaphoreType.DMA((13,)), pltpu.SemaphoreType.DMA((2,)),
        pltpu.SemaphoreType.DMA((2,)), pltpu.SemaphoreType.DMA((2, 3, 2)),
        pltpu.SemaphoreType.DMA((2, 3, 2)), pltpu.SemaphoreType.DMA((2,)),
    ]
    out = jax.ShapeDtypeStruct((toks, cols), BF16)
    heads = cols // width
    flat, by_head = pltpu.VMEM((toks, cols), BF16), pltpu.VMEM((heads, toks, width), BF16)
    staged = pl.pallas_call(
        functools.partial(kernel, ny, nz, nx, toks, width, feats),
        out_shape=(flat, by_head, by_head, by_head),
        in_specs=[pl.BlockSpec(memory_space=pl.ANY)] * 6,
        out_specs=(pl.BlockSpec(memory_space=pltpu.VMEM),) * 4,
        scratch_shapes=scratch,
        compiler_params=pltpu.CompilerParams(collective_id=0, has_side_effects=True),
    )(queries, key_vectors, value_vectors, feature_proj, out_weight, grad_output)
    return pl.pallas_call(
        functools.partial(write_out, heads, width),
        out_shape=(out,) * 4,
        in_specs=[pl.BlockSpec(memory_space=pl.ANY)] * 4,
        compiler_params=pltpu.CompilerParams(vmem_limit_bytes=1 << 20),
        out_specs=(pl.BlockSpec(memory_space=pl.ANY),) * 4,
        scratch_shapes=[pltpu.SemaphoreType.DMA((1 + 3 * heads,))],
    )(*staged)


def solution(mesh):
    rows = P("seq", "head")
    return jax.shard_map(
        local,
        mesh=mesh,
        in_specs=(rows, rows, rows, P("head", None, None), P("head", None), rows),
        out_specs=(rows,) * 4,
        check_vma=False,
    )
```

time: 49.2 us -> 48.4 us (0.984)
  Pallas kernels: 48.4 us -> 47.6 us
    pallas_call x1, Pallas kernels: 47.6 us -> 46.7 us  [local(): pl.pallas_call(functools.partial(kernel, ny, nz, nx, toks, width, feats),...]
where the time goes in v3:
time: 48.4 us; the launch traced here: 48.2 us
  Pallas kernels  47.6 us (98%)
  between operations  0.64 us (1%)
    pallas_call x1, Pallas kernels, local(): pl.pallas_call(functools.partial(kernel, ny, nz, nx, toks, width, feats),...  46.7 us

profile of v3, /device:TPU:1, one launch (start us, length us, event | category | flops | bytes accessed | tf_op | source)
XLA Modules:
  0.0 48.2 jit_solution(12731730044112842954)
XLA Ops:
  0.6 46.7 %shard_map.93 = (bf16[128,512]{1,0:T(8,128)(2,1)S(1)}, bf16[4,128,128]{2,1,0:T(8,128)(2,1)S(1)}, bf16[4,128,128]{2,1,0:T(8,128)(2,1)S(1)}, bf16[4,128,128]{2,1,0:T(8,128)(2,1)S(1)}) custom-call(bf16[128,512]{1,0:T(8,128)(2,1)} %refs_0_.1, bf16[128,512]{1,0:T(8,128)(2,1)} %refs_1_.1, bf16[128,512]{1,0:T(8,128)(2,1)} %refs_2_.1, bf16[4,128,256]{2,1,0:T(8,128)(2,1)} %refs_3_.1, ...), custom_call_target="tpu_custom_call" | custom-call | tf_op jit(solution)/shard_map/pallas_call | solution.py:457
  47.3 0.9 %shard_map.94 = (bf16[128,512]{1,0:T(8,128)(2,1)}, bf16[128,512]{1,0:T(8,128)(2,1)}, bf16[128,512]{1,0:T(8,128)(2,1)}, bf16[128,512]{1,0:T(8,128)(2,1)}) custom-call(bf16[128,512]{1,0:T(8,128)(2,1)S(1)} %get-tuple-element.8.lo, bf16[4,128,128]{2,1,0:T(8,128)(2,1)S(1)} %get-tuple-element.9.gq, bf16[4,128,128]{2,1,0:T(8,128)(2,1)S(1)} %get-tuple-element.10.gk, ...), custom_call_target="tpu_custom_call" | custom-call | tf_op jit(solution)/shard_map/pallas_call | solution.py:465
